TPU v7x, 32 devices: a whole 2x2x4 slice. The times are simulated.
32 devices in a mesh: slab: 8 (over z, x), depth: 4 (over y, core).
Axes of the slice: x: 2, y: 2, z: 4, core: 2. Of those that a mesh axis runs over, the one named last changes fastest.
Arguments:
- right_side: float32 [3, 8, 8, 32, 256], P(None, None, 'slab', 'depth'), may hold values from -4 to 9
- smoother: float32 [3, 8, 32, 256], P(None, 'slab', 'depth'), may hold values from 0.1 to 1
- material: int32 [8, 32, 256], P('slab', 'depth'), may hold values from 0 to 15
- moduli: float32 [16], replicated, may hold values from 0.25 to 4
- element_matrix: float32 [24, 24], replicated, may hold values from -0.15 to 3, as said below
- coarse_inverse: float32 [24, 24], replicated, may hold values from -0.2 to 1.2, as said below
- surface_map: int32 [8, 256], P('slab'), may hold values from 0 to 2047, as said below
- line_of_sight: float32 [3, 8, 256], P(None, 'slab'), may hold values from -3 to 3
Outputs:
- residual: float32 [3, 8, 8, 32, 256], P(None, None, 'slab', 'depth')
- pixels: float32 [8, 2048], P('depth', 'slab')
Inputs may be any that keep to these rules, and one draw needn't show every extreme that they name: `element_matrix`: symmetric. `coarse_inverse`: symmetric. `surface_map`: pixel p lies in tile p // 256. At most 64 surface nodes of one slab block lie in one tile, and some tile holds exactly 64 surface nodes of every slab block.
All inputs are finite; a program needn't handle non-finite values.
Results may differ from a plain program's by a relative error of at most 0.0003.
Values sent between devices are 32-bit elements; how exact they have to be, the bound alone decides.
No kernel may reach another device: no remote copies, remote signals or barrier semaphores. Data moves between devices by JAX's collectives and lax.ppermute only.
A program may use at most 64 MiB of HBM per device.

v0:
```python
import jax
import jax.numpy as jnp
from jax import lax
from jax.sharding import PartitionSpec as P

PIX = 256


def extended(array, sides, width):
    for axis, dim in sides:
        peers, length = (lax.axis_size(axis), array.shape[dim])
        up = [(i, (i + 1) % peers) for i in range(peers - 1)]
        down = [(j, i) for i, j in up]
        last = lax.slice_in_dim(array, length - width, length, axis=dim)
        initial = lax.slice_in_dim(array, 0, width, axis=dim)
        before = lax.ppermute(last, axis, up)
        after = lax.ppermute(initial, axis, down)
        array = jnp.concatenate([before, array, after], axis=dim)
    return array


def broadcast(value, axis, source):
    kept = jnp.where(lax.axis_index(axis) == source, value, 0).astype(value.dtype)
    return lax.psum(kept, axis)


def stiffness(padded_field, padded_moduli, element_matrix):
    sources = padded_field.shape[1]
    span_x = padded_field.shape[2] - 1
    span_z = padded_field.shape[3] - 1
    span_y = padded_moduli.shape[2]
    corners = []
    for corner in range(8):
        along_x, along_z, along_y = (corner // 4, corner // 2 % 2, corner % 2)
        corners.append(
            padded_field[
                :,
                :,
                along_x : along_x + span_x,
                along_z : along_z + span_z,
                along_y : along_y + span_y,
            ]
        )
    stacked = jnp.stack(corners, 0).reshape(24, -1)
    forces = jnp.dot(
        element_matrix, stacked, precision=lax.Precision.HIGHEST, preferred_element_type=jnp.float32
    )
    forces = forces.reshape(8, 3, sources, span_x, span_z, span_y) * padded_moduli[1:, 1:, :]
    forces = jnp.pad(forces, ((0, 0), (0, 0), (0, 0), (0, 0), (0, 0), (0, 1)))
    summed = jnp.zeros((3, sources, span_x - 1, span_z - 1, span_y), jnp.float32)
    for corner in range(8):
        along_x, along_z, along_y = (corner // 4, corner // 2 % 2, corner % 2)
        summed = (
            summed
            + forces[
                corner,
                :,
                :,
                1 - along_x : 1 - along_x + span_x - 1,
                1 - along_z : 1 - along_z + span_z - 1,
                1 - along_y : 1 - along_y + span_y,
            ]
        )
    return summed


def pack_slots(values, targets, n_slab):
    node_count = values.shape[1]
    capacity = 2 * node_count // n_slab
    tile_owner = targets // PIX
    in_tile = targets % PIX
    onehot = (tile_owner[:, None] == jnp.arange(n_slab, dtype=jnp.int32)[None]).astype(jnp.int32)
    slot_rank = jnp.sum((jnp.cumsum(onehot, axis=0) - 1) * onehot, axis=1)
    send_vals = (
        jnp.zeros((values.shape[0], capacity, n_slab), jnp.float32)
        .at[:, slot_rank, tile_owner]
        .set(values)
    )
    send_ids = (
        jnp.zeros((1, capacity, n_slab), jnp.float32)
        .at[0, slot_rank, tile_owner]
        .set(in_tile.astype(jnp.float32))
    )
    return (send_vals, send_ids)


def bin_pixels(got_vals, got_ids):
    pixel_index = got_ids.reshape(-1).astype(jnp.int32)
    rows = got_vals.shape[0]
    return jnp.zeros((rows, PIX), jnp.float32).at[:, pixel_index].add(got_vals.reshape(rows, -1))


def body(
    right_side,
    smoother,
    material,
    moduli,
    element_matrix,
    coarse_inverse,
    surface_map,
    line_of_sight,
):
    components, sources, width_x, width_z, width_y = right_side.shape
    n_slab = lax.axis_size("slab")
    n_depth = lax.axis_size("depth")
    slab_rank = lax.axis_index("slab")
    depth_rank = lax.axis_index("depth")
    levels = jnp.arange(moduli.shape[0], dtype=jnp.int32)
    modulus_field = jnp.sum(
        jnp.where(material[None] == levels[:, None, None, None], moduli[:, None, None, None], 0.0),
        axis=0,
    )
    weights = smoother[:, None]
    stacked = jnp.concatenate(
        [
            right_side.reshape(components * sources, width_x, width_z, width_y),
            smoother,
            modulus_field[None],
        ],
        0,
    )
    source_pad = extended(stacked, (("slab", 1), ("depth", 2)), 1)
    agg_nodes = float(width_x * width_z * n_depth * width_y)
    block_sums = jnp.sum(right_side, axis=(2, 3, 4))
    placed = jnp.where(
        jnp.arange(n_slab, dtype=jnp.int32)[:, None, None] == slab_rank, block_sums[None], 0.0
    )
    placed = placed.reshape(components * n_slab, sources)
    coarse_sum = lax.psum(placed, ("slab", "depth"))
    coarse_vec = coarse_sum / agg_nodes
    correction = jnp.dot(
        coarse_inverse,
        coarse_vec,
        precision=lax.Precision.HIGHEST,
        preferred_element_type=jnp.float32,
    )
    by_block = correction.reshape(n_slab, components, sources)
    own_corr = lax.dynamic_index_in_dim(by_block, slab_rank, 0, keepdims=False)
    direction = weights * right_side + own_corr[:, :, None, None, None]
    numerator = lax.psum(jnp.sum(right_side * direction, axis=(0, 2, 3, 4)), ("slab", "depth"))
    field_pad = source_pad[: components * sources].reshape(
        components, sources, width_x + 2, width_z + 2, width_y
    )
    weight_pad = source_pad[components * sources : components * sources + components]
    moduli_pad = source_pad[components * sources + components]
    low_block = jnp.maximum(slab_rank - 1, 0)
    high_block = jnp.minimum(slab_rank + 1, n_slab - 1)
    low_corr = jnp.where(
        slab_rank > 0, lax.dynamic_index_in_dim(by_block, low_block, 0, keepdims=False), 0.0
    )
    high_corr = jnp.where(
        slab_rank < n_slab - 1,
        lax.dynamic_index_in_dim(by_block, high_block, 0, keepdims=False),
        0.0,
    )
    row_corr = jnp.concatenate([low_corr[None], own_corr[None], high_corr[None]], 0)
    row_corr = jnp.transpose(row_corr, (1, 2, 0))
    depth_mask = jnp.ones((width_z + 2,), jnp.float32)
    depth_mask = depth_mask.at[0].set(jnp.where(depth_rank > 0, 1.0, 0.0))
    depth_mask = depth_mask.at[width_z + 1].set(jnp.where(depth_rank < n_depth - 1, 1.0, 0.0))
    padded = (
        weight_pad[:, None] * field_pad
        + row_corr[:, :, :, None, None] * depth_mask[None, None, None, :, None]
    )
    padded = jnp.pad(padded, ((0, 0), (0, 0), (0, 0), (0, 0), (1, 0)))
    applied = stiffness(padded, moduli_pad, element_matrix)
    denominator = lax.psum(jnp.sum(direction * applied, axis=(0, 2, 3, 4)), ("slab", "depth"))
    step_size = numerator / denominator
    residual = right_side - step_size[None, :, None, None, None] * applied
    surface = step_size[None, :, None, None] * direction[:, :, :, width_z - 1, :]
    projected = jnp.sum(line_of_sight[:, None] * surface, axis=0).reshape(sources, -1)
    projected = broadcast(projected, "depth", n_depth - 1)
    targets = surface_map.reshape(-1)
    per_row = sources // n_depth
    send_vals, send_ids = pack_slots(projected, targets, n_slab)
    got_vals, got_ids = (
        lax.all_to_all(send_vals, "slab", split_axis=2, concat_axis=2, tiled=True),
        lax.all_to_all(send_ids, "slab", split_axis=2, concat_axis=2, tiled=True),
    )
    binned = bin_pixels(got_vals, got_ids)
    pixels = lax.dynamic_slice_in_dim(binned, depth_rank * per_row, per_row, 0)
    return (residual, pixels)


def solution(mesh):
    return jax.shard_map(
        body,
        mesh=mesh,
        in_specs=(
            P(None, None, "slab", "depth", None),
            P(None, "slab", "depth", None),
            P("slab", "depth", None),
            P(),
            P(),
            P(),
            P("slab", None),
            P(None, "slab", None),
        ),
        out_specs=(P(None, None, "slab", "depth", None), P("depth", "slab")),
        check_vma=False,
    )
```

profile of v0, /device:TPU:0, one launch (start us, length us, event | category | flops | bytes accessed | tf_op | source)
XLA Modules:
  0.0 215.8 jit_solution(9086493570849835887)
XLA Ops:
  2.5 1.3 collective-permute-start.1
  3.8 5.5 %collective-permute-start = (f32[28,1,8,256]{3,2,1,0:T(8,128)S(1)}, f32[28,1,8,256]{3,2,1,0:T(8,128)S(1)}, u32[]{:S(2)}, u32[]{:S(2)}) collective-permute-start(f32[28,1,8,256]{3,2,1,0:T(8,128)S(1)} %pad_maximum_fusion.1), channel_id=1, source_target_pairs={{0,4},{4,8},{8,12},{12,16},{16,20},{20,24},{24,28},{1,5},{5,9},{9,... | collective-permute-start | bytes 688136 | tf_op jit(solution)/shard_map/ppermute | solution.py:16
  12.9 38.7 %scatter_fusion = f32[64,8]{0,1:T(8,128)} fusion(f32[64,8]{0,1:T(8,128)} %broadcast.316, s32[256]{0:T(256)S(1)} %bitcast.120, f32[256]{0:T(256)S(1)} %get-tuple-element.49), kind=kCustom, calls=%fused_computation | custom fusion | bytes 5120 | tf_op jit(solution)/shard_map/scatter | solution.py:82
  51.6 6.2 %all-to-all-start = ((f32[1,64,8]{1,0,2:T(1,128)}), f32[1,64,8]{1,0,2:T(1,128)S(1)}, u32[]{:S(2)}, u32[]{:S(2)}) async-start(f32[1,64,8]{1,0,2:T(1,128)} %bitcast.34), calls=%async_computation | async-start | bytes 8192 | tf_op jit(solution)/shard_map/all_to_all | solution.py:178
  57.8 1.1 reduce_sum.56
  59.2 40.8 %psum.28 = f32[24,8]{1,0:T(8,128)S(1)} all-reduce(f32[24,8]{1,0:T(8,128)S(1)} %broadcast_select_fusion), channel_id=1, replica_groups=mesh['slab'=8,'depth'=4] {'slab','depth'}, use_global_device_ids=true, to_apply=%region_1.2 | all-reduce | flops 192 | bytes 1536 | tf_op jit(solution)/shard_map/psum | solution.py:129
  101.7 1.3 copy.99
  104.1 1.3 collective-permute-start.2
  105.4 1.3 collective-permute-start.3
  107.3 3.9 %collective-permute-done.3 = f32[28,3,1,256]{3,2,1,0:T(1,128)S(1)} collective-permute-done((f32[28,3,1,256]{3,2,1,0:T(1,128)S(1)}, f32[28,3,1,256]{3,2,1,0:T(1,128)S(1)}, u32[]{:S(2)}, u32[]{:S(2)}) %collective-permute-start.3) | collective-permute-done | bytes 86048 | tf_op jit(solution)/shard_map/ppermute | solution.py:17
  112.4 1.1 fusion.1
  114.6 1.2 fusion.3
  116.7 1.1 fusion.5
  118.8 1.2 fusion.7
  121.0 3.8 %reshape.438 = f32[24,36864]{1,0:T(8,128)S(1)} reshape(f32[8,3,8,2,9,256]{5,4,3,2,1,0:T(8,128)} %fusion.8) | data formatting | bytes 7077888 | tf_op jit(solution)/shard_map/reshape | solution.py:44
  124.8 4.9 %convolution_bitcast_fusion = f32[24,36864]{1,0:T(8,128)} fusion(f32[24,36864]{1,0:T(8,128)S(1)} %reshape.438, f32[24,24]{1,0:T(8,128)S(1)} %copy-done), kind=kOutput, calls=%fused_computation.3 | convolution fusion | flops 254803968 | bytes 7080192 | tf_op jit(solution)/shard_map/dot_general | solution.py:45
  129.8 5.2 %reshape.439 = f32[8,3,8,2,9,256]{5,4,3,2,1,0:T(8,128)} reshape(f32[24,36864]{1,0:T(8,128)} %convolution_bitcast_fusion) | data formatting | bytes 7077888 | tf_op jit(solution)/shard_map/reshape | solution.py:48
  135.0 3.6 %broadcast_multiply_fusion = f32[8,3,8,2,9,256]{5,4,3,2,1,0:T(8,128)S(1)} fusion(f32[8,3,8,2,9,256]{5,4,3,2,1,0:T(8,128)} %reshape.439, f32[2,9,256]{2,1,0:T(8,128)S(1)} %copy-done.5), kind=kLoop, calls=%fused_computation.8 | loop fusion | flops 884736 | bytes 7096320 | tf_op jit(solution)/shard_map/mul | solution.py:48
  139.1 40.8 %all-reduce.3 = (f32[8]{0:T(128)S(1)}, f32[8]{0:T(128)S(1)}) all-reduce(f32[8]{0:T(128)S(1)} %get-tuple-element.39, f32[8]{0:T(128)S(1)} %get-tuple-element.38), channel_id=1, replica_groups=mesh['slab'=8,'depth'=4] {'slab','depth'}, use_global_device_ids=true, to_apply=%region_3.4 | all-reduce | flops 16 | bytes 128 | tf_op jit(solution)/shard_map/psum | solution.py:140
  180.1 6.7 %psum.31 = f32[8,256]{1,0:T(8,128)S(1)} all-reduce(f32[8,256]{1,0:T(8,128)S(1)} %broadcast_select_fusion.1), channel_id=1, replica_groups=mesh['slab'=8,'depth'=4] {'depth'}, use_global_device_ids=true, to_apply=%region_12.13 | all-reduce | flops 2048 | bytes 16384 | tf_op jit(solution)/shard_map/psum | solution.py:24
  187.0 11.6 %scatter_fusion.1 = f32[8,64,8]{0,2,1:T(8,128)S(1)} fusion(f32[8,64,8]{0,2,1:T(8,128)S(1)} %broadcast_in_dim.103, s32[256]{0:T(256)S(1)} %bitcast.121, f32[256,8]{1,0:T(8,128)S(1)} %copy.81), kind=kCustom, calls=%fused_computation.1 | custom fusion | bytes 26624 | tf_op jit(solution)/shard_map/scatter | solution.py:77
  199.5 4.3 %all-to-all-start.1 = ((f32[8,1,512]{2,1,0:T(1,128)}), f32[8,1,512]{2,1,0:T(1,128)S(1)}, u32[]{:S(2)}, u32[]{:S(2)}) async-start(f32[8,1,512]{2,1,0:T(1,128)} %reshape.473), calls=%async_computation.1 | async-start | bytes 32768 | tf_op jit(solution)/shard_map/all_to_all | solution.py:177
  204.5 5.8 %all-to-all-done.1 = f32[8,1,512]{2,1,0:T(1,128)S(1)} async-done(((f32[8,1,512]{2,1,0:T(1,128)}), f32[8,1,512]{2,1,0:T(1,128)S(1)}, u32[]{:S(2)}, u32[]{:S(2)}) %all-to-all-start.1) | async-done | bytes 16416 | tf_op jit(solution)/shard_map/all_to_all | solution.py:177
  212.1 2.9 %scatter_custom_fusion.2 = f32[8,256]{0,1:T(8,128)S(1)} fusion(s32[512]{0:T(512)} %bitcast.145, f32[512,8]{1,0:T(8,128)S(1)} %copy.85, f32[]{:T(128)} %constant.114.clone.1), kind=kCustom, calls=%fused_computation.57 | custom fusion | flops 4096 | bytes 8704 | tf_op jit(solution)/shard_map/scatter-add | solution.py:90
  (81 shorter events, 18.9 us)
Async XLA Ops:
  0.6 124.2 %copy-start = (f32[24,24]{1,0:T(8,128)S(1)}, f32[24,24]{1,0:T(8,128)}, u32[]{:S(2)}) copy-start(f32[24,24]{1,0:T(8,128)} %param.16) | copy-start | bytes 6916
  0.6 110.5 %copy-start.3 = (f32[3,1,8,256]{3,2,1,0:T(8,128)S(1)}, f32[3,1,8,256]{3,2,1,0:T(8,128)}, u32[]{:S(2)}) copy-start(f32[3,1,8,256]{3,2,1,0:T(8,128)} %param.13) | copy-start | bytes 73732
  0.7 102.6 %copy-start.1 = (f32[3,8,1,8,256]{4,3,2,1,0:T(8,128)S(1)}, f32[3,8,1,8,256]{4,3,2,1,0:T(8,128)}, u32[]{:S(2)}) copy-start(f32[3,8,1,8,256]{4,3,2,1,0:T(8,128)} %param.12) | copy-start | bytes 589828
  2.5 100.7 %collective-permute-start.1 = (f32[28,1,8,256]{3,2,1,0:T(8,128)S(1)}, f32[28,1,8,256]{3,2,1,0:T(8,128)S(1)}, u32[]{:S(2)}, u32[]{:S(2)}) collective-permute-start(f32[28,1,8,256]{3,2,1,0:T(8,128)S(1)} %pad_maximum_fusion.1), channel_id=1, source_target_pairs={{4,0},{8,4},{12,8},{16,12},{20,16},{24,20},{28,24},{5,1},{9,5},{13... | collective-permute-start | bytes 688136 | tf_op jit(solution)/shard_map/ppermute | solution.py:17
  3.8 99.4 %collective-permute-start = (f32[28,1,8,256]{3,2,1,0:T(8,128)S(1)}, f32[28,1,8,256]{3,2,1,0:T(8,128)S(1)}, u32[]{:S(2)}, u32[]{:S(2)}) collective-permute-start(f32[28,1,8,256]{3,2,1,0:T(8,128)S(1)} %pad_maximum_fusion.1), channel_id=1, source_target_pairs={{0,4},{4,8},{8,12},{12,16},{16,20},{20,24},{24,28},{1,5},{5,9},{9,... | collective-permute-start | bytes 688136 | tf_op jit(solution)/shard_map/ppermute | solution.py:16
  51.6 51.4 %all-to-all-start = ((f32[1,64,8]{1,0,2:T(1,128)}), f32[1,64,8]{1,0,2:T(1,128)S(1)}, u32[]{:S(2)}, u32[]{:S(2)}) async-start(f32[1,64,8]{1,0,2:T(1,128)} %bitcast.34), calls=%async_computation | async-start | bytes 8192 | tf_op jit(solution)/shard_map/all_to_all | solution.py:178
  101.0 0.6 copy-start.6
  104.1 3.1 %collective-permute-start.2 = (f32[28,3,1,256]{3,2,1,0:T(1,128)S(1)}, f32[28,3,1,256]{3,2,1,0:T(1,128)S(1)}, u32[]{:S(2)}, u32[]{:S(2)}) collective-permute-start(f32[28,3,1,256]{3,2,1,0:T(1,128)S(1)} %get-tuple-element.43), channel_id=1, source_target_pairs={{0,1},{1,2},{2,3},{4,5},{5,6},{6,7},{8,9},{9,10},{10,11},{12,13},{... | collective-permute-start | bytes 258056 | tf_op jit(solution)/shard_map/ppermute | solution.py:16
  105.4 5.7 %collective-permute-start.3 = (f32[28,3,1,256]{3,2,1,0:T(1,128)S(1)}, f32[28,3,1,256]{3,2,1,0:T(1,128)S(1)}, u32[]{:S(2)}, u32[]{:S(2)}) collective-permute-start(f32[28,3,1,256]{3,2,1,0:T(1,128)S(1)} %get-tuple-element.44), channel_id=1, source_target_pairs={{1,0},{2,1},{3,2},{5,4},{6,5},{7,6},{9,8},{10,9},{11,10},{13,12},{... | collective-permute-start | bytes 258056 | tf_op jit(solution)/shard_map/ppermute | solution.py:17
  129.8 5.2 %copy-start.5 = (f32[2,9,256]{2,1,0:T(8,128)S(1)}, f32[2,9,256]{2,1,0:T(8,128)}, u32[]{:S(2)}) copy-start(f32[2,9,256]{2,1,0:T(8,128)} %slice.139) | copy-start | bytes 55300
  135.0 3.7 %copy-start.2 = (f32[3,8,1,8,256]{4,3,2,1,0:T(8,128)S(1)}, f32[3,8,1,8,256]{4,3,2,1,0:T(8,128)}, u32[]{:S(2)}) copy-start(f32[3,8,1,8,256]{4,3,2,1,0:T(8,128)} %param.12) | copy-start | bytes 589828
  135.0 3.7 %copy-start.4 = (f32[3,1,8,256]{3,2,1,0:T(8,128)S(1)}, f32[3,1,8,256]{3,2,1,0:T(8,128)}, u32[]{:S(2)}) copy-start(f32[3,1,8,256]{3,2,1,0:T(8,128)} %param.13) | copy-start | bytes 73732
  135.0 3.7 %copy-start.7 = (f32[1,3,8]{2,1,0:T(4,128)S(1)}, f32[1,3,8]{2,1,0:T(4,128)}, u32[]{:S(2)}) copy-start(f32[1,3,8]{2,1,0:T(4,128)} %copy-done.6) | copy-start | bytes 292
  138.7 41.3 %copy-start.8 = (f32[3,1,256]{2,0,1:T(4,128)S(1)}, f32[3,1,256]{2,0,1:T(4,128)}, u32[]{:S(2)}) copy-start(f32[3,1,256]{2,0,1:T(4,128)} %copy.99) | copy-start | bytes 9220
  199.5 10.9 %all-to-all-start.1 = ((f32[8,1,512]{2,1,0:T(1,128)}), f32[8,1,512]{2,1,0:T(1,128)S(1)}, u32[]{:S(2)}, u32[]{:S(2)}) async-start(f32[8,1,512]{2,1,0:T(1,128)} %reshape.473), calls=%async_computation.1 | async-start | bytes 32768 | tf_op jit(solution)/shard_map/all_to_all | solution.py:177
where the time goes:
time: 218 us; the launch traced here: 216 us
  blocking collectives  88.4 us (41%)
  local copies, waits for them, and re-layouts  74.5 us (34%)
  starting transfers between devices  19.9 us (9%)
  other arithmetic  16.4 us (8%)
  waiting for transfers between devices  9.68 us (4%)
  matrix products  5.84 us (3%)
    psum x1, blocking collectives, body(): lax.psum(jnp.sum(right_side * direction, axis=(0, 2, 3, 4)), ('slab', 'de...  40.8 us
    psum x1, blocking collectives, body(): coarse_sum = lax.psum(placed, ('slab', 'depth'))  40.8 us
    scatter x1, local copies, waits for them, and re-layouts, pack_slots(): send_ids = jnp.zeros((1, capacity, n_slab), jnp.float32).at[0, slot_rank,...  38.7 us
    scatter x2, local copies, waits for them, and re-layouts, pack_slots(): send_vals = jnp.zeros((values.shape[0], capacity, n_slab), jnp.float32).a...  11.7 us
    unnamed x29, local copies, waits for them, and re-layouts  10.8 us
    ppermute x2, starting transfers between devices, extended(): before = lax.ppermute(last, axis, up)  6.81 us
    psum x1, blocking collectives, broadcast(): return lax.psum(kept, axis)  6.75 us
    all_to_all x1, starting transfers between devices, body(): lax.all_to_all(send_ids, 'slab', split_axis=2, concat_axis=2, tiled=True)  6.2 us
  transfers between devices with their start and end apart: 6, of which 2 were waited for; matrix products, arithmetic and copies ran while one was open for 22% of the time, Pallas kernels for 0%

commit v1 on v0

v1 whole, which is shorter than its diff:
```python
import jax
import jax.numpy as jnp
from jax import lax
from jax.experimental import pallas as pl
from jax.experimental.pallas import tpu as pltpu
from jax.sharding import PartitionSpec as P

PIX = 256
LANES = 128
F32 = jnp.float32
BF16 = jnp.bfloat16

AT_NUM = 24
AT_DEN = 32
AT_LOW = 40
AT_OWN = 64
AT_MOD = 88


def iota(shape, dim):
    return lax.broadcasted_iota(jnp.int32, shape, dim)


def dot(a, b):
    return lax.dot_general(
        a, b, (((1,), (0,)), ((), ())), precision=lax.Precision.HIGHEST, preferred_element_type=F32
    )


def dot_t(a, b):
    return lax.dot_general(
        a, b, (((1,), (1,)), ((), ())), precision=lax.Precision.HIGHEST, preferred_element_type=F32
    )


def dot_b(a, b):
    return lax.dot_general(a, b, (((1,), (0,)), ((), ())), preferred_element_type=F32)


def dot_bt(a, b):
    return lax.dot_general(a, b, (((1,), (1,)), ((), ())), preferred_element_type=F32)


def split2(x):
    high = x.astype(BF16)
    low = (x - high.astype(F32)).astype(BF16)
    return high, low


def split3(x):
    high = x.astype(BF16)
    rest = x - high.astype(F32)
    mid = rest.astype(BF16)
    low = (rest - mid.astype(F32)).astype(BF16)
    return high, mid, low


def onehot(mask):
    return jnp.where(mask, 1.0, 0.0)


def next_lane(x, lane):
    return jnp.where(lane == x.shape[1] - 1, 0.0, pltpu.roll(x, x.shape[1] - 1, 1))


def prev_lane(x, lane):
    return jnp.where(lane == 0, 0.0, pltpu.roll(x, 1, 1))


def to_halves(ref, halves):
    for h, half in enumerate(halves):
        half[...] = ref[:, h * LANES : (h + 1) * LANES]


def strided(halves, start, rows, stride):
    return jnp.concatenate([half[pl.ds(start, rows, stride=stride), :] for half in halves], 1)


def weigh_kernel(comps, srcs, wz, r_ref, s_ref, u_ref, top_ref, part_ref, *halves):
    rows = comps * srcs
    to_halves(r_ref, halves)
    acc_r = acc_ru = None
    for z in range(wz):
        force = strided(halves, z, rows, wz)
        weight = jnp.concatenate(
            [
                jnp.broadcast_to(s_ref[m * wz + z : m * wz + z + 1, :], (srcs, force.shape[1]))
                for m in range(comps)
            ],
            0,
        )
        u = force * weight
        u_ref[z * rows : (z + 1) * rows, :] = u
        acc_r = force if z == 0 else acc_r + force
        acc_ru = force * u if z == 0 else acc_ru + force * u
    top_ref[...] = u
    part_ref[:rows, :] = acc_r
    part_ref[rows:, :] = sum(acc_ru[m * srcs : (m + 1) * srcs] for m in range(comps))


def corner_of(index):
    return (index // 2 % 2) * 4 + (index // 4) * 2 + index % 2


def prepare_kernel(
    comps, srcs, n_slab, n_depth, cap, k_ref, top_ref, los_ref, map_ref, kh_ref, kl_ref, g_ref, pack_ref, y_ref
):
    size = 8 * comps
    full = size * srcs
    k_high, k_low = split2(k_ref[...])
    group = iota((full, size), 0) // srcs
    spread = onehot(corner_of(group // comps) * comps + group % comps == iota((full, size), 1)).astype(BF16)
    same = iota((full, full), 0) % srcs == iota((full, full), 1) % srcs
    for part, out in ((k_high, kh_ref), (k_low, kl_ref)):
        wide = dot_b(spread, part).astype(BF16)
        out[...] = jnp.where(same, dot_bt(wide, spread), 0.0).astype(BF16)
    block = comps * n_slab
    col = iota((block, size), 1)
    row_m = iota((block, size), 0) % comps
    corner = col // comps
    own = iota((block, block), 0) // comps
    other = iota((block, block), 1) // comps
    for v in range(4):
        keep = (col % comps == row_m) & ((corner // 2 % 2 == 1) | (v // 2 == 0))
        keep = keep & ((corner % 2 == 1) | (v % 2 == 0))
        low = onehot(keep & (corner // 4 == 0))
        high = onehot(keep & (corner // 4 == 1))
        k_lo, k_hi = dot(low, k_ref[...]), dot(high, k_ref[...])
        g_ref[2 * v * block : (2 * v + 1) * block, :] = jnp.where(
            other == own, dot_t(k_hi, high), jnp.where(other == own - 1, dot_t(k_hi, low), 0.0)
        )
        g_ref[(2 * v + 1) * block : (2 * v + 2) * block, :] = jnp.where(
            other == own, dot_t(k_lo, low), jnp.where(other == own + 1, dot_t(k_lo, high), 0.0)
        )
    nodes = map_ref.shape[1]
    tile = map_ref[...] // PIX
    per_row = srcs // n_depth
    los = los_ref[...]
    value = sum(los[m : m + 1, :] * top_ref[m * srcs : (m + 1) * srcs, :] for m in range(comps))
    y_ref[...] = jnp.zeros(y_ref.shape, F32)
    y_ref[:srcs, :] = value
    y_ref[srcs : srcs + comps, :] = los
    y_ref[srcs + comps : srcs + comps + 1, :] = (map_ref[...] % PIX).astype(F32)
    n_rows = 4 * n_depth
    row = iota((n_rows, y_ref.shape[0]), 0)
    pick = iota((n_rows, y_ref.shape[0]), 1)
    kind = row % 4
    first = jnp.where(kind == 1, row // 4 * per_row, jnp.where(kind == 2, srcs, srcs + 2))
    wide = jnp.concatenate(
        [dot(onehot((pick == first + a) & (kind > 0)), y_ref[...]) for a in range(2)], 1
    )
    parts = jnp.concatenate(split3(wide), 0)
    owner = onehot(iota((max(n_slab, 8), nodes), 0) == tile)
    before = onehot(iota((nodes, nodes), 0) < iota((nodes, nodes), 1)).astype(BF16)
    rank = jnp.sum(dot_b(owner.astype(BF16), before) * owner, 0, keepdims=True).astype(jnp.int32)
    lane = iota((LANES, nodes), 0)

    def one_tile(t, carry):
        here = jnp.where(tile == t, rank, -LANES)
        match = jnp.concatenate([onehot(lane == here), onehot(lane == here + cap)], 1).astype(BF16)
        got = dot_bt(parts, match)
        pack_ref[pl.ds(pl.multiple_of(t * n_rows, n_rows), n_rows), :] = (
            got[:n_rows] + got[n_rows : 2 * n_rows] + got[2 * n_rows :]
        )
        return carry

    lax.fori_loop(0, n_slab, one_tile, 0, unroll=n_slab <= 8)


def element_kernel(
    comps,
    srcs,
    wz,
    rank_ref,
    moduli_ref,
    material_ref,
    own_ref,
    left_ref,
    below_ref,
    corner_ref,
    part_ref,
    kh_ref,
    kl_ref,
    pack_ref,
    acc_ref,
    side_ref,
    down_ref,
    diag_ref,
    send_ref,
    uf_ref,
    uh_ref,
    ul_ref,
    z_ref,
):
    rows = comps * srcs
    width = own_ref.shape[1]
    lane = iota((rows, width), 1)
    inner = rank_ref[1] > 0
    material = material_ref[...]
    modulus = jnp.zeros(material.shape, F32)
    for level in range(moduli_ref.shape[0]):
        modulus = jnp.where(material == level, moduli_ref[level], modulus)
    side_ref[wz * rows :, :] = modulus
    down_ref[rows:, :] = modulus
    diag_ref[rows:, :] = modulus
    for z in range(-1, wz):
        for x in range(2):
            if z < 0:
                u = (corner_ref, below_ref)[x][...]
            else:
                u = (left_ref, own_ref)[x][z * rows : (z + 1) * rows, :]
            for y, value in enumerate((prev_lane(u, lane), u)):
                at = (((z + 1) * 2 + x) * 2 + y) * rows
                high, low = split2(value)
                uf_ref[at : at + rows, :] = value
                uh_ref[at : at + rows, :] = high
                ul_ref[at : at + rows, :] = low
    k_high, k_low = kh_ref[...], kl_ref[...]
    full = 8 * rows
    energy = jnp.zeros((rows, width), F32)
    sums = [jnp.zeros((rows, width), F32), jnp.zeros((rows, width), F32)]
    outs = (side_ref, acc_ref)
    edge = (diag_ref, down_ref)
    held = [None, None]
    for k in range(wz):
        at = k * 4 * rows
        u_high = uh_ref[at : at + full, :]
        force = dot_b(k_high, u_high) + dot_b(k_high, ul_ref[at : at + full, :]) + dot_b(k_low, u_high)
        force = force * modulus[k : k + 1, :]
        for c in range(8):
            energy = energy + force[c * rows : (c + 1) * rows] * uf_ref[at + c * rows : at + (c + 1) * rows, :]
        for x in range(2):
            def at_nodes(z):
                c = (z * 2 + x) * 2
                return force[(c + 1) * rows : (c + 2) * rows] + next_lane(force[c * rows : (c + 1) * rows], lane)

            lower, upper = at_nodes(0), at_nodes(1)
            if k == 0:
                edge[x][:rows, :] = lower
                sums[x] = sums[x] + jnp.where(inner, lower, 0.0) + upper
            else:
                outs[x][(k - 1) * rows : k * rows, :] = held[x] + lower
                sums[x] = sums[x] + lower + upper
            held[x] = upper
    for x in range(2):
        outs[x][(wz - 1) * rows : wz * rows, :] = held[x]
    z_ref[...] = jnp.zeros(z_ref.shape, F32)
    z_ref[:AT_DEN, :] = part_ref[...]
    z_ref[AT_DEN:AT_LOW, :] = sum(energy[m * srcs : (m + 1) * srcs] for m in range(comps))
    z_ref[AT_LOW : AT_LOW + rows, :] = sums[0]
    z_ref[AT_OWN : AT_OWN + rows, :] = sums[1]
    zrow = iota(modulus.shape, 0)
    bad = (zrow == 0) & jnp.logical_not(inner)
    good_sum = jnp.sum(jnp.where(bad, 0.0, modulus), 0, keepdims=True)
    bad_sum = jnp.sum(jnp.where(bad, modulus, 0.0), 0, keepdims=True)
    pick = jnp.where(iota((8, width), 0) // 2 == 0, good_sum, bad_sum)
    at_start = iota((8, width), 1) == 0
    pick = jnp.where(at_start == (iota((8, width), 0) % 2 == 1), pick, 0.0)
    z_ref[AT_MOD : AT_MOD + 8, :] = jnp.where(iota((8, width), 0) < 4, pick, 0.0)
    total = dot_t(jnp.ones((8, width), F32), z_ref[...])
    pack = pack_ref[...]
    send_ref[...] = jnp.where(
        iota(pack.shape, 0) % 4 == 0, jnp.broadcast_to(total[:1], pack.shape), pack
    )


def finish_kernel(
    comps,
    srcs,
    wz,
    n_slab,
    n_depth,
    cap,
    agg,
    rank_ref,
    got_ref,
    r_ref,
    acc_ref,
    mod_ref,
    side_ref,
    down_ref,
    diag_ref,
    kh_ref,
    kl_ref,
    g_ref,
    ci_ref,
    res_ref,
    pix_ref,
    c_ref,
    *halves,
):
    rows = comps * srcs
    width = r_ref.shape[1]
    n_dev = n_slab * n_depth
    block = comps * n_slab
    slab = rank_ref[0]
    depth = rank_ref[1]
    parts = got_ref[pl.ds(0, n_dev, stride=4), :]
    from_dev = iota((block, n_dev), 1) // n_depth
    to_slab = iota((block, n_dev), 0) // comps
    here = dot(onehot(from_dev == to_slab), parts)
    after = dot(onehot(from_dev == to_slab + 1), parts)
    total = dot(jnp.ones((8, n_dev), F32), parts)
    lane = iota((block, LANES), 1)
    comp = iota((block, LANES), 0) % comps
    lane8 = iota((8, LANES), 1)

    def own_lanes(start):
        return (lane >= start + comp * srcs) & (lane < start + (comp + 1) * srcs)

    stacked = jnp.concatenate(
        [
            jnp.where(own_lanes(0), here, 0.0),
            jnp.where(own_lanes(AT_OWN), here, 0.0) + jnp.where(own_lanes(AT_LOW), after, 0.0),
            jnp.where((lane8 >= AT_NUM) & (lane8 < AT_NUM + srcs), total, 0.0),
            jnp.where((lane8 >= AT_DEN) & (lane8 < AT_DEN + srcs), total, 0.0),
        ],
        0,
    )
    fold = onehot(iota((LANES, srcs), 0) % srcs == iota((LANES, srcs), 1))
    folded = dot(stacked, fold)
    sums = folded[:block]
    linear = folded[block : 2 * block]
    num = folded[2 * block : 2 * block + 1]
    den = folded[2 * block + 8 : 2 * block + 9]
    coarse = jnp.zeros((block, block), F32)
    for v in range(4):
        at = AT_MOD + v
        coarse = coarse + here[:, at : at + 1] * g_ref[2 * v * block : (2 * v + 1) * block, :]
        coarse = coarse + after[:, at : at + 1] * g_ref[(2 * v + 1) * block : (2 * v + 2) * block, :]
    corr = dot(ci_ref[...], sums / agg)
    num = num + jnp.sum(corr * sums, 0, keepdims=True)
    den = den + jnp.sum(corr * (2.0 * linear + dot(coarse, corr)), 0, keepdims=True)
    step = num / den
    step_col = jnp.sum(
        jnp.where(
            iota((rows, srcs), 0) % srcs == iota((rows, srcs), 1), jnp.broadcast_to(step, (rows, srcs)), 0.0
        ),
        1,
        keepdims=True,
    )
    which = iota((3 * rows, block), 0)
    source = iota((3 * rows, block), 1)
    near = onehot(
        (source % comps == which % rows // srcs) & (source // comps == slab - 1 + which // rows)
    )
    near = dot(near, corr)
    near = jnp.sum(
        jnp.where(iota((3 * rows, srcs), 0) % srcs == iota((3 * rows, srcs), 1), near, 0.0), 1, keepdims=True
    )
    full = 8 * rows
    stack = []
    for e in range(2):
        pieces = [near[(e + c // 2 % 2) * rows : (e + c // 2 % 2 + 1) * rows] for c in range(8)]
        stack.append(jnp.broadcast_to(jnp.concatenate(pieces, 0), (full, LANES)))
    lane_f = iota((full, LANES), 1)
    corner = iota((full, LANES), 0) // rows
    field = jnp.where(lane_f // 4 == 0, stack[0], jnp.where(lane_f // 4 == 1, stack[1], 0.0))
    field = jnp.where((corner // 4 == 0) & (lane_f // 2 % 2 == 1), 0.0, field)
    field = jnp.where((corner % 2 == 0) & (lane_f % 2 == 1), 0.0, field)
    f_high, f_low = split2(field)
    k_high = kh_ref[...]
    q = dot_b(k_high, f_high) + dot_b(k_high, f_low) + dot_b(kl_ref[...], f_high)
    at_start = iota((rows, width), 1) == 0

    def coefficient(e, z, y, edge):
        at = ((z * 2 + 1 - e) * 2 + y) * rows
        piece = q[at : at + rows]
        value = jnp.broadcast_to(piece[:, e * 4 + edge : e * 4 + edge + 1], (rows, width))
        if y == 1:
            other = jnp.broadcast_to(piece[:, e * 4 + edge + 1 : e * 4 + edge + 2], (rows, width))
            value = jnp.where(at_start, other, value)
        return value

    base = {(e, z, y): coefficient(e, z, y, 0) for e in range(2) for z in range(2) for y in range(2)}
    first = dict(base)
    for e in range(2):
        for y in range(2):
            first[e, 1, y] = jnp.where(depth == 0, coefficient(e, 1, y, 2), base[e, 1, y])
    mods = {}
    lane_m = iota((8, width), 1)
    for e in range(2):
        main = (mod_ref[rows:, :], side_ref[wz * rows :, :])[e]
        edge = (down_ref, diag_ref)[e][rows:, :]
        for y in range(2):
            a, b = (main, edge) if y == 1 else (next_lane(main, lane_m), next_lane(edge, lane_m))
            mods[e, y] = [a[k : k + 1, :] for k in range(wz)] + [b[:1, :]]
    to_halves(r_ref, halves)
    for z in range(wz):
        applied = acc_ref[z * rows : (z + 1) * rows, :] + side_ref[z * rows : (z + 1) * rows, :]
        if z == wz - 1:
            applied = applied + down_ref[:rows, :] + diag_ref[:rows, :]
        table = first if z == 0 else base
        for (e, up, y), value in table.items():
            applied = applied + value * mods[e, y][z + 1 - up]
        change = step_col * applied
        for h, half in enumerate(halves):
            at = pl.ds(z, rows, stride=wz)
            half[at, :] = half[at, :] - change[:, h * LANES : (h + 1) * LANES]
    for h, half in enumerate(halves):
        res_ref[:, h * LANES : (h + 1) * LANES] = half[...]
    per_row = srcs // n_depth
    slots = [got_ref[pl.ds((n_depth - 1) * 4 + j, n_slab, stride=4 * n_depth), :] for j in range(1, 4)]
    lane_s = iota((n_slab, LANES), 1)
    head = lane_s < cap

    def head_twice(x):
        return jnp.where(head, x, pltpu.roll(x, cap, 1))

    def tail_twice(x):
        return jnp.where(head, pltpu.roll(x, LANES - cap, 1), x)

    sight = (head_twice(slots[1]), tail_twice(slots[1]), head_twice(slots[2]))
    ids = tail_twice(slots[2])
    lane_e = iota((srcs, LANES), 1)
    mine = onehot(
        (iota((srcs, LANES), 0) == depth * per_row + lane_e // cap) & (lane_e < per_row * cap)
    )
    c_ref[...] = dot(corr, mine)
    value = slots[0]
    for m in range(comps):
        value = value + sight[m] * c_ref[pl.ds(m, n_slab, stride=comps), :]
    value = value * dot(jnp.broadcast_to(step, (8, srcs)), mine)[:1]
    value = jnp.where(lane_s < per_row * cap, value, 0.0)
    binned = jnp.zeros((24, PIX), F32)
    row8 = iota((8, LANES), 0)
    half = iota((8, LANES), 1) // cap
    pixel = iota((PIX, LANES), 0).astype(F32)
    for s in range(n_slab):
        vals = jnp.where(row8 == half, jnp.broadcast_to(value[s : s + 1], (8, LANES)), 0.0)
        match = onehot(pixel == ids[s : s + 1]).astype(BF16)
        binned = binned + dot_bt(jnp.concatenate(split3(vals), 0), match)
    binned = binned[:8] + binned[8:16] + binned[16:]
    pix_ref[...] = binned[:per_row]


def call(kernel, outs, scratch=(), name=None):
    def run(*args):
        specs = [
            pl.BlockSpec(memory_space=pltpu.SMEM if a.ndim == 1 else pltpu.VMEM) for a in args
        ]
        return pl.pallas_call(
            kernel,
            out_shape=[jax.ShapeDtypeStruct(s, d) for s, d in outs],
            in_specs=specs,
            out_specs=[pl.BlockSpec(memory_space=pltpu.VMEM)] * len(outs),
            scratch_shapes=[pltpu.VMEM(s, d) for s, d in scratch],
            name=name,
        )(*args)

    return run


def bind(kernel, *static):
    def run(*refs):
        kernel(*static, *refs)

    return run


def body(
    right_side,
    smoother,
    material,
    moduli,
    element_matrix,
    coarse_inverse,
    surface_map,
    line_of_sight,
):
    comps, srcs, width_x, wz, wy = right_side.shape
    n_slab = lax.axis_size("slab")
    n_depth = lax.axis_size("depth")
    if width_x != 1 or srcs != 8 or comps != 3 or wz != 8 or srcs // n_depth != 2:
        raise ValueError("unsupported shape")
    rows = comps * srcs
    n_dev = n_slab * n_depth
    block = comps * n_slab
    cap = 2 * width_x * wy // n_slab
    agg = float(width_x * wz * n_depth * wy)
    ranks = jnp.stack([lax.axis_index("slab"), lax.axis_index("depth")]).astype(jnp.int32)
    force = right_side.reshape(rows * wz, wy)

    up = [(s * n_depth + d, (s + 1) * n_depth + d + 1) for s in range(n_slab - 1) for d in range(n_depth - 1)]
    down = [(b, a) for a, b in up]
    slab_up = [(i, i + 1) for i in range(n_slab - 1)]
    slab_down = [(b, a) for a, b in slab_up]
    depth_up = [(i, i + 1) for i in range(n_depth - 1)]
    depth_down = [(b, a) for a, b in depth_up]
    both = ("slab", "depth")

    u, top, part = call(
        bind(weigh_kernel, comps, srcs, wz),
        [((wz * rows, wy), F32), ((rows, wy), F32), ((rows + srcs, wy), F32)],
        [((rows * wz, LANES), F32)] * (wy // LANES),
        name="weigh",
    )(force, smoother.reshape(comps * wz, wy))
    below = lax.ppermute(top, "depth", depth_up)
    corner = lax.ppermute(top, both, up)
    left = lax.ppermute(u, "slab", slab_up)
    k_high, k_low, g_parts, pack = call(
        bind(prepare_kernel, comps, srcs, n_slab, n_depth, cap),
        [
            ((8 * rows, 8 * rows), BF16),
            ((8 * rows, 8 * rows), BF16),
            ((8 * block, block), F32),
            ((4 * n_dev, LANES), F32),
        ],
        [((16, wy), F32)],
        name="prepare",
    )(element_matrix, top, line_of_sight.reshape(comps, wy), surface_map.reshape(1, wy))
    acc, side, below_force, diag, send = call(
        bind(element_kernel, comps, srcs, wz),
        [
            ((wz * rows, wy), F32),
            ((wz * rows + 8, wy), F32),
            ((rows + 8, wy), F32),
            ((rows + 8, wy), F32),
            ((4 * n_dev, LANES), F32),
        ],
        [
            ((4 * (wz + 1) * rows, wy), F32),
            ((4 * (wz + 1) * rows, wy), BF16),
            ((4 * (wz + 1) * rows, wy), BF16),
            ((LANES, wy), F32),
        ],
        name="elements",
    )(ranks, moduli, material.reshape(wz, wy), u, left, below, corner, part, k_high, k_low, pack)
    got = lax.all_to_all(send.reshape(n_dev, 4, LANES), both, 0, 0, tiled=True)
    side_got = lax.ppermute(side, "slab", slab_down)
    down_got = lax.ppermute(below_force, "depth", depth_down)
    diag_got = lax.ppermute(diag, both, down)
    residual, pixels = call(
        bind(finish_kernel, comps, srcs, wz, n_slab, n_depth, cap, agg),
        [((rows * wz, wy), F32), ((srcs // n_depth, PIX), F32)],
        [((block, LANES), F32)] + [((rows * wz, LANES), F32)] * (wy // LANES),
        name="finish",
    )(
        ranks,
        got.reshape(4 * n_dev, LANES),
        force,
        acc,
        below_force,
        side_got,
        down_got,
        diag_got,
        k_high,
        k_low,
        g_parts,
        coarse_inverse,
    )
    return (residual.reshape(right_side.shape), pixels)


def solution(mesh):
    return jax.shard_map(
        body,
        mesh=mesh,
        in_specs=(
            P(None, None, "slab", "depth", None),
            P(None, "slab", "depth", None),
            P("slab", "depth", None),
            P(),
            P(),
            P(),
            P("slab", None),
            P(None, "slab", None),
        ),
        out_specs=(P(None, None, "slab", "depth", None), P("depth", "slab")),
        check_vma=False,
    )
```

time: 218 us -> 41.9 us (0.19)
  blocking collectives: 88.4 us -> 0 us
  local copies, waits for them, and re-layouts: 74.5 us -> 2.06 us
  other arithmetic: 16.4 us -> 0.58 us
  Pallas kernels: 0 us -> 11.8 us
  matrix products: 5.84 us -> 0 us
  waiting for transfers between devices: 9.68 us -> 4.79 us
    psum x3 -> x0, blocking collectives: 88.4 us -> none  [the longest x1 40.8 us: body(): lax.psum(jnp.sum(right_side * direction, axis=(0, 2, 3, 4)), ('slab', 'de...]
    scatter x5 -> x0, local copies, waits for them, and re-layouts: 50.5 us -> none  [the longest x1 38.7 us: pack_slots(): send_ids = jnp.zeros((1, capacity, n_slab), jnp.float32).at[0, slot_rank,...]
    pallas_call x0 -> x4, Pallas kernels: none -> 11.8 us  [run(): pl.pallas_call(kernel, out_shape=[jax.ShapeDtypeStruct(s, d) for s, d in...]
    reshape x5 -> x0, local copies, waits for them, and re-layouts: 9.3 us -> none  [the longest x1 5.23 us: stiffness(): forces.reshape(8, 3, sources, span_x, span_z, span_y)]
    unnamed x29 -> x21, local copies, waits for them, and re-layouts: 10.8 us -> 2.06 us
    dot_general x2 -> x0, matrix products: 5.84 us -> none  [the longest x1 4.95 us: stiffness(): jnp.dot(element_matrix, stacked, precision=lax.Precision.HIGHEST, preferr...]
    ppermute x4 -> x6, starting transfers between devices: 9.39 us -> 15.2 us  [the longest x1 4.87 us: body(): left = lax.ppermute(u, 'slab', slab_up)]
    all_to_all x2 -> x1, starting transfers between devices: 10.5 us -> 5.95 us  [body(): got = lax.all_to_all(send.reshape(n_dev, 4, LANES), both, 0, 0, tiled=True)]
  transfers between devices with their start and end apart: 6 -> 7, of which waited for: 2 -> 2; matrix products, arithmetic and copies ran while one was open for 22% -> 3% of each run, Pallas kernels for 0% -> 8%
where the time goes in v1:
time: 41.9 us; the launch traced here: 41.2 us
  starting transfers between devices  21.1 us (50%)
  Pallas kernels  11.8 us (28%)
  waiting for transfers between devices  4.79 us (11%)
  local copies, waits for them, and re-layouts  2.06 us (5%)
  between operations  0.78 us (2%)
  other arithmetic  0.58 us (1%)
    pallas_call x4, Pallas kernels, run(): pl.pallas_call(kernel, out_shape=[jax.ShapeDtypeStruct(s, d) for s, d in...  11.8 us
    all_to_all x1, starting transfers between devices, body(): got = lax.all_to_all(send.reshape(n_dev, 4, LANES), both, 0, 0, tiled=True)  5.95 us
    ppermute x1, starting transfers between devices, body(): left = lax.ppermute(u, 'slab', slab_up)  4.87 us
    ppermute x1, starting transfers between devices, body(): below = lax.ppermute(top, 'depth', depth_up)  3.82 us
    ppermute x1, waiting for transfers between devices, body(): diag_got = lax.ppermute(diag, both, down)  2.67 us
    ppermute x1, starting transfers between devices, body(): corner = lax.ppermute(top, both, up)  2.6 us
    all_to_all x1, waiting for transfers between devices, body(): got = lax.all_to_all(send.reshape(n_dev, 4, LANES), both, 0, 0, tiled=True)  2.11 us
    unnamed x21, local copies, waits for them, and re-layouts  2.06 us
  transfers between devices with their start and end apart: 7, of which 2 were waited for; matrix products, arithmetic and copies ran while one was open for 3% of the time, Pallas kernels for 8%

profile of v1, /device:TPU:0, one launch (start us, length us, event | category | flops | bytes accessed | tf_op | source)
XLA Modules:
  0.0 41.2 jit_solution(10201694210271390050)
XLA Ops:
  0.6 1.7 %weigh.1 = (f32[192,256]{1,0:T(8,128)}, f32[24,256]{1,0:T(8,128)}, f32[32,256]{1,0:T(8,128)}) custom-call(f32[192,256]{1,0:T(8,128)} %bitcast.13, f32[24,256]{1,0:T(8,128)} %bitcast.17), custom_call_target="tpu_custom_call" | custom-call | tf_op jit(solution)/shard_map/weigh/pallas_call | solution.py:442
  2.3 4.9 %collective-permute-start = (f32[192,256]{1,0:T(8,128)}, f32[192,256]{1,0:T(8,128)S(1)}, u32[]{:S(2)}, u32[]{:S(2)}) collective-permute-start(f32[192,256]{1,0:T(8,128)} %get-tuple-element.16.refs_3_), channel_id=1, source_target_pairs={{0,4},{4,8},{8,12},{12,16},{16,20},{20,24},{24,28},{1,5},{5,9},{9,... | collective-permute-start | bytes 589832 | tf_op jit(solution)/shard_map/ppermute | solution.py:500
  7.2 2.6 %collective-permute-start.2 = (f32[24,256]{1,0:T(8,128)}, f32[24,256]{1,0:T(8,128)S(1)}, u32[]{:S(2)}, u32[]{:S(2)}) collective-permute-start(f32[24,256]{1,0:T(8,128)} %get-tuple-element.17.refs_1_), channel_id=1, source_target_pairs={{0,5},{1,6},{2,7},{4,9},{5,10},{6,11},{8,13},{9,14},{10,15},{12,17... | collective-permute-start | bytes 73736 | tf_op jit(solution)/shard_map/ppermute | solution.py:499
  9.8 3.8 %collective-permute-start.1 = (f32[24,256]{1,0:T(8,128)}, f32[24,256]{1,0:T(8,128)S(1)}, u32[]{:S(2)}, u32[]{:S(2)}) collective-permute-start(f32[24,256]{1,0:T(8,128)} %get-tuple-element.17.refs_1_), channel_id=1, source_target_pairs={{0,1},{1,2},{2,3},{4,5},{5,6},{6,7},{8,9},{9,10},{10,11},{12,13},{... | collective-permute-start | bytes 73736 | tf_op jit(solution)/shard_map/ppermute | solution.py:498
  13.6 0.0 copy-start.8
  13.6 0.6 %pad_add_fusion.refs_0_ = s32[2]{0:T(128)} fusion(s32[1]{0:T(128)} %bitcast.1, s32[1]{0:T(128)} %bitcast), kind=kLoop, calls=%fused_computation.1 | loop fusion | flops 2 | bytes 16 | tf_op jit(solution)/shard_map/stack | solution.py:481
  14.2 0.1 copy-done.8
  14.3 0.6 %copy.13 = f32[3,1,256]{2,0,1:T(4,128)} copy(f32[3,1,256]{2,1,0:T(1,128)S(1)} %copy-done.8) | data formatting | bytes 6144
  14.9 3.4 %prepare.1 = (bf16[192,192]{1,0:T(8,128)(2,1)}, bf16[192,192]{1,0:T(8,128)(2,1)}, f32[192,24]{1,0:T(8,128)}, f32[128,128]{1,0:T(8,128)}) custom-call(f32[24,24]{1,0:T(8,128)} %refs_0_.1, f32[24,256]{1,0:T(8,128)} %get-tuple-element.17.refs_1_, f32[3,256]{1,0:T(4,128)} %bitcast.18, s32[1,256]{1,0:T(1,128)} %refs_3_.1), custom_call_target="tpu_custom_call" | custom-call | tf_op jit(solution)/shard_map/prepare/pallas_call | solution.py:442
  18.3 0.0 collective-permute-done.2.refs_6_
  18.3 0.0 collective-permute-done.1.refs_5_
  18.4 0.6 %copy-done.6 = f32[24,256]{1,0:T(8,128)} copy-done((f32[24,256]{1,0:T(8,128)}, f32[24,256]{1,0:T(8,128)S(1)}, u32[]{:S(2)}) %copy-start.6) | copy-done | bytes 24600
  18.9 0.0 copy-done.7
  19.0 0.1 copy-done.2
  19.0 3.1 %elements.1 = (f32[192,256]{1,0:T(8,128)}, f32[200,256]{1,0:T(8,128)}, f32[32,256]{1,0:T(8,128)}, f32[32,256]{1,0:T(8,128)}, f32[128,128]{1,0:T(8,128)}) custom-call(s32[2]{0:T(128)} %pad_add_fusion.refs_0_, f32[16]{0:T(128)} %refs_1_.1, s32[8,256]{1,0:T(8,128)} %bitcast.19, f32[192,256]{1,0:T(8,128)} %get-tuple-element.16.refs_3_, f32[192,256]{1,0:T(8,128)} %copy-done.2, ...), custom_call_target="tpu_custom_call" | custom-call | tf_op jit(solution)/shard_map/elements/pallas_call | solution.py:442
  22.1 1.3 %collective-permute-start.3 = (f32[200,256]{1,0:T(8,128)}, f32[200,256]{1,0:T(8,128)S(1)}, u32[]{:S(2)}, u32[]{:S(2)}) collective-permute-start(f32[200,256]{1,0:T(8,128)} %get-tuple-element.25), channel_id=1, source_target_pairs={{4,0},{8,4},{12,8},{16,12},{20,16},{24,20},{28,24},{5,1},{9,5},{13... | collective-permute-start | bytes 614408 | tf_op jit(solution)/shard_map/ppermute | solution.py:530
  23.4 5.9 %all-to-all-start = ((f32[32,4,128]{2,1,0:T(4,128)}), f32[32,4,128]{2,1,0:T(4,128)S(1)}, u32[]{:S(2)}, u32[]{:S(2)}) async-start(f32[32,4,128]{2,1,0:T(4,128)} %bitcast.16), calls=%async_computation | async-start | bytes 131072 | tf_op jit(solution)/shard_map/all_to_all | solution.py:529
  29.4 1.3 %collective-permute-start.5 = (f32[32,256]{1,0:T(8,128)S(1)}, f32[32,256]{1,0:T(8,128)S(1)}, u32[]{:S(2)}, u32[]{:S(2)}) collective-permute-start(f32[32,256]{1,0:T(8,128)S(1)} %copy-done.9), channel_id=1, source_target_pairs={{5,0},{6,1},{7,2},{9,4},{10,5},{11,6},{13,8},{14,9},{15,10},{17,12... | collective-permute-start | bytes 98312 | tf_op jit(solution)/shard_map/ppermute | solution.py:532
  30.7 1.3 %collective-permute-start.4 = (f32[32,256]{1,0:T(8,128)S(1)}, f32[32,256]{1,0:T(8,128)S(1)}, u32[]{:S(2)}, u32[]{:S(2)}) collective-permute-start(f32[32,256]{1,0:T(8,128)S(1)} %copy-done.3), channel_id=1, source_target_pairs={{1,0},{2,1},{3,2},{5,4},{6,5},{7,6},{9,8},{10,9},{11,10},{13,12},{... | collective-permute-start | bytes 98312 | tf_op jit(solution)/shard_map/ppermute | solution.py:531
  32.0 2.7 %collective-permute-done.5.refs_7_ = f32[32,256]{1,0:T(8,128)S(1)} collective-permute-done((f32[32,256]{1,0:T(8,128)S(1)}, f32[32,256]{1,0:T(8,128)S(1)}, u32[]{:S(2)}, u32[]{:S(2)}) %collective-permute-start.5) | collective-permute-done | bytes 32800 | tf_op jit(solution)/shard_map/ppermute | solution.py:532
  34.6 2.1 %all-to-all-done = f32[32,4,128]{2,1,0:T(4,128)S(1)} async-done(((f32[32,4,128]{2,1,0:T(4,128)}), f32[32,4,128]{2,1,0:T(4,128)S(1)}, u32[]{:S(2)}, u32[]{:S(2)}) %all-to-all-start) | async-done | bytes 65568 | tf_op jit(solution)/shard_map/all_to_all | solution.py:529
  36.8 0.6 %copy-done = f32[32,4,128]{2,1,0:T(4,128)} copy-done((f32[32,4,128]{2,1,0:T(4,128)}, f32[32,4,128]{2,1,0:T(4,128)S(1)}, u32[]{:S(2)}) %copy-start) | copy-done | bytes 65560
  37.4 0.1 copy-done.1
  37.5 3.7 %finish.1 = (f32[192,256]{1,0:T(8,128)}, f32[2,256]{1,0:T(2,128)}) custom-call(s32[2]{0:T(128)} %pad_add_fusion.refs_0_, f32[128,128]{1,0:T(8,128)} %bitcast.15, f32[192,256]{1,0:T(8,128)} %bitcast.14, f32[192,256]{1,0:T(8,128)} %get-tuple-element.23.refs_3_, f32[32,256]{1,0:T(8,128)} %get-tuple-element.24.refs_4_, f32[200,256]{1,0:T(8,128)} %copy-done.1, ...), custom_call_target="tpu_custom_call" | custom-call | tf_op jit(solution)/shard_map/finish/pallas_call | solution.py:442
  (16 shorter events, 0.0 us)
Async XLA Ops:
  2.3 16.1 %collective-permute-start = (f32[192,256]{1,0:T(8,128)}, f32[192,256]{1,0:T(8,128)S(1)}, u32[]{:S(2)}, u32[]{:S(2)}) collective-permute-start(f32[192,256]{1,0:T(8,128)} %get-tuple-element.16.refs_3_), channel_id=1, source_target_pairs={{0,4},{4,8},{8,12},{12,16},{16,20},{20,24},{24,28},{1,5},{5,9},{9,... | collective-permute-start | bytes 589832 | tf_op jit(solution)/shard_map/ppermute | solution.py:500
  7.2 11.2 %collective-permute-start.2 = (f32[24,256]{1,0:T(8,128)}, f32[24,256]{1,0:T(8,128)S(1)}, u32[]{:S(2)}, u32[]{:S(2)}) collective-permute-start(f32[24,256]{1,0:T(8,128)} %get-tuple-element.17.refs_1_), channel_id=1, source_target_pairs={{0,5},{1,6},{2,7},{4,9},{5,10},{6,11},{8,13},{9,14},{10,15},{12,17... | collective-permute-start | bytes 73736 | tf_op jit(solution)/shard_map/ppermute | solution.py:499
  9.8 8.5 %collective-permute-start.1 = (f32[24,256]{1,0:T(8,128)}, f32[24,256]{1,0:T(8,128)S(1)}, u32[]{:S(2)}, u32[]{:S(2)}) collective-permute-start(f32[24,256]{1,0:T(8,128)} %get-tuple-element.17.refs_1_), channel_id=1, source_target_pairs={{0,1},{1,2},{2,3},{4,5},{5,6},{6,7},{8,9},{9,10},{10,11},{12,13},{... | collective-permute-start | bytes 73736 | tf_op jit(solution)/shard_map/ppermute | solution.py:498
  13.6 0.7 %copy-start.8 = (f32[3,1,256]{2,1,0:T(1,128)S(1)}, f32[3,1,256]{2,1,0:T(1,128)}, u32[]{:S(2)}) copy-start(f32[3,1,256]{2,1,0:T(1,128)} %param.15) | copy-start | bytes 9220
  18.3 0.6 %copy-start.6 = (f32[24,256]{1,0:T(8,128)}, f32[24,256]{1,0:T(8,128)S(1)}, u32[]{:S(2)}) copy-start(f32[24,256]{1,0:T(8,128)S(1)} %collective-permute-done.2.refs_6_) | copy-start | bytes 73732
  18.3 0.6 %copy-start.7 = (f32[24,256]{1,0:T(8,128)}, f32[24,256]{1,0:T(8,128)S(1)}, u32[]{:S(2)}) copy-start(f32[24,256]{1,0:T(8,128)S(1)} %collective-permute-done.1.refs_5_) | copy-start | bytes 73732
  18.4 0.7 %copy-start.2 = (f32[192,256]{1,0:T(8,128)}, f32[192,256]{1,0:T(8,128)S(1)}, u32[]{:S(2)}) copy-start(f32[192,256]{1,0:T(8,128)S(1)} %collective-permute-done.refs_4_) | copy-start | bytes 589828
  22.1 14.7 %collective-permute-start.3 = (f32[200,256]{1,0:T(8,128)}, f32[200,256]{1,0:T(8,128)S(1)}, u32[]{:S(2)}, u32[]{:S(2)}) collective-permute-start(f32[200,256]{1,0:T(8,128)} %get-tuple-element.25), channel_id=1, source_target_pairs={{4,0},{8,4},{12,8},{16,12},{20,16},{24,20},{28,24},{5,1},{9,5},{13... | collective-permute-start | bytes 614408 | tf_op jit(solution)/shard_map/ppermute | solution.py:530
  23.4 6.0 %copy-start.9 = (f32[32,256]{1,0:T(8,128)S(1)}, f32[32,256]{1,0:T(8,128)}, u32[]{:S(2)}) copy-start(f32[32,256]{1,0:T(8,128)} %get-tuple-element.26) | copy-start | bytes 98308
  23.4 7.3 %copy-start.3 = (f32[32,256]{1,0:T(8,128)S(1)}, f32[32,256]{1,0:T(8,128)}, u32[]{:S(2)}) copy-start(f32[32,256]{1,0:T(8,128)} %get-tuple-element.24.refs_4_) | copy-start | bytes 98308
  23.4 13.4 %all-to-all-start = ((f32[32,4,128]{2,1,0:T(4,128)}), f32[32,4,128]{2,1,0:T(4,128)S(1)}, u32[]{:S(2)}, u32[]{:S(2)}) async-start(f32[32,4,128]{2,1,0:T(4,128)} %bitcast.16), calls=%async_computation | async-start | bytes 131072 | tf_op jit(solution)/shard_map/all_to_all | solution.py:529
  29.4 5.3 %collective-permute-start.5 = (f32[32,256]{1,0:T(8,128)S(1)}, f32[32,256]{1,0:T(8,128)S(1)}, u32[]{:S(2)}, u32[]{:S(2)}) collective-permute-start(f32[32,256]{1,0:T(8,128)S(1)} %copy-done.9), channel_id=1, source_target_pairs={{5,0},{6,1},{7,2},{9,4},{10,5},{11,6},{13,8},{14,9},{15,10},{17,12... | collective-permute-start | bytes 98312 | tf_op jit(solution)/shard_map/ppermute | solution.py:532
  30.7 4.0 %collective-permute-start.4 = (f32[32,256]{1,0:T(8,128)S(1)}, f32[32,256]{1,0:T(8,128)S(1)}, u32[]{:S(2)}, u32[]{:S(2)}) collective-permute-start(f32[32,256]{1,0:T(8,128)S(1)} %copy-done.3), channel_id=1, source_target_pairs={{1,0},{2,1},{3,2},{5,4},{6,5},{7,6},{9,8},{10,9},{11,10},{13,12},{... | collective-permute-start | bytes 98312 | tf_op jit(solution)/shard_map/ppermute | solution.py:531
  34.6 2.1 %copy-start.4 = (f32[32,256]{1,0:T(8,128)}, f32[32,256]{1,0:T(8,128)S(1)}, u32[]{:S(2)}) copy-start(f32[32,256]{1,0:T(8,128)S(1)} %collective-permute-done.5.refs_7_) | copy-start | bytes 98308
  34.6 2.1 %copy-start.5 = (f32[32,256]{1,0:T(8,128)}, f32[32,256]{1,0:T(8,128)S(1)}, u32[]{:S(2)}) copy-start(f32[32,256]{1,0:T(8,128)S(1)} %collective-permute-done.4.refs_6_) | copy-start | bytes 98308
  36.8 0.6 %copy-start = (f32[32,4,128]{2,1,0:T(4,128)}, f32[32,4,128]{2,1,0:T(4,128)S(1)}, u32[]{:S(2)}) copy-start(f32[32,4,128]{2,1,0:T(4,128)S(1)} %all-to-all-done) | copy-start | bytes 196612
  36.8 0.7 %copy-start.1 = (f32[200,256]{1,0:T(8,128)}, f32[200,256]{1,0:T(8,128)S(1)}, u32[]{:S(2)}) copy-start(f32[200,256]{1,0:T(8,128)S(1)} %collective-permute-done.3.refs_5_) | copy-start | bytes 614404
